TPU v7x, 256 devices: a whole 4x4x8 slice. The times are simulated.
256 devices in a mesh: seq: 32 (over x, y, core), head: 8 (over z).
Axes of the slice: x: 4, y: 4, z: 8, core: 2. Of those that a mesh axis runs over, the one named last changes fastest.
Arguments:
- queries: bfloat16 [32768, 32, 128], P(('seq', 'head')), may hold values from -48 to 48
- keys_in: bfloat16 [32768, 32, 128], P(('seq', 'head')), may hold values from -48 to 48
- values: bfloat16 [32768, 32, 128], P(('seq', 'head')), may hold values from -48 to 48
- cotangent: bfloat16 [32768, 32, 128], P(('seq', 'head')), may hold values from -48 to 48
Outputs:
- attended: bfloat16 [32768, 32, 128], P('seq', 'head')
- grad_queries: bfloat16 [32768, 32, 128], P('seq', 'head')
- grad_keys: bfloat16 [32768, 32, 128], P('seq', 'head')
- grad_values: bfloat16 [32768, 32, 128], P('seq', 'head')
All inputs are finite; a program needn't handle non-finite values.
Results may differ from a plain program's by a relative error of at most 0.01.
Values may be sent and summed in bfloat16 or wider, within the bound.
A program may use at most 128 MiB of HBM per device.

v0:
```python
import jax
import jax.numpy as jnp
from jax import lax
from jax.sharding import PartitionSpec as P

BLOCK = 512
OFFSET = 1048576


def entering(x, axis, combine, identity, reverse):
    count, index = (lax.axis_size(axis), lax.axis_index(axis))
    everything = lax.all_gather(x.astype(jnp.bfloat16), axis)
    start = jnp.broadcast_to(jnp.asarray(identity, x.dtype), x.shape)

    def step(k, before):
        at = count - 1 - k if reverse else k
        reached = at > index if reverse else at < index
        new = combine(before, everything[at].astype(x.dtype))
        return jnp.where(reached, new, before)

    return lax.fori_loop(0, count, step, start)


def add_states(earlier, later):
    return jax.tree.map(jnp.add, earlier, later)


def masked_scores(left_side, right_side, causal_mask):
    raw_scores = jnp.einsum(
        "thd,shd->hts", left_side, right_side, preferred_element_type=jnp.float32
    )
    return jnp.where(causal_mask[None], raw_scores, 0.0).astype(jnp.bfloat16)


def block_outputs(
    query_rows, key_rows, value_rows, grad_rows, position, state_before, state_after, causal_mask
):
    before_used = state_before.astype(jnp.bfloat16)
    after_used = state_after.astype(jnp.bfloat16)
    attention = masked_scores(query_rows, key_rows, causal_mask)
    grad_scores = masked_scores(grad_rows, value_rows, causal_mask)
    result = jnp.einsum("thd,hde->the", query_rows, before_used, preferred_element_type=jnp.float32)
    result = result + jnp.einsum(
        "hts,she->the", attention, value_rows, preferred_element_type=jnp.float32
    )
    result = (result / position[:, None, None]).astype(jnp.bfloat16)
    grad_query = jnp.einsum(
        "the,hde->thd", grad_rows, before_used, preferred_element_type=jnp.float32
    )
    grad_query = grad_query + jnp.einsum(
        "hts,shd->thd", grad_scores, key_rows, preferred_element_type=jnp.float32
    )
    grad_key = jnp.einsum(
        "she,hde->shd", value_rows, after_used, preferred_element_type=jnp.float32
    )
    grad_key = grad_key + jnp.einsum(
        "hts,thd->shd", grad_scores, query_rows, preferred_element_type=jnp.float32
    )
    grad_value = jnp.einsum(
        "shd,hde->she", key_rows, after_used, preferred_element_type=jnp.float32
    )
    grad_value = grad_value + jnp.einsum(
        "hts,the->she", attention, grad_rows, preferred_element_type=jnp.float32
    )
    return (
        result,
        grad_query.astype(jnp.bfloat16),
        grad_key.astype(jnp.bfloat16),
        grad_value.astype(jnp.bfloat16),
    )


def local_work(inputs):
    queries = inputs[0][:, 0]
    keys_in = inputs[1][:, 0]
    values = inputs[2][:, 0]
    cotangent = inputs[3][:, 0]
    row_count, head_count, head_width = queries.shape
    my_index = lax.axis_index("seq")
    position = (my_index * row_count + jnp.arange(row_count, dtype=jnp.int32) + OFFSET + 1).astype(
        jnp.float32
    )
    scaled_grad = (cotangent.astype(jnp.float32) / position[:, None, None]).astype(jnp.bfloat16)
    block_count = row_count // BLOCK
    block_shape = (block_count, BLOCK, head_count, head_width)
    query_blocks = queries.reshape(block_shape)
    key_blocks = keys_in.reshape(block_shape)
    value_blocks = values.reshape(block_shape)
    grad_blocks = scaled_grad.reshape(block_shape)
    block_kv = jnp.einsum(
        "nshd,nshe->nhde", key_blocks, value_blocks, preferred_element_type=jnp.float32
    )
    block_qg = jnp.einsum(
        "nthd,nthe->nhde", query_blocks, grad_blocks, preferred_element_type=jnp.float32
    )
    own_kv = jnp.sum(block_kv, 0)
    own_qg = jnp.sum(block_qg, 0)
    zero_state = jnp.zeros((head_count, head_width, head_width), jnp.float32)
    prefix_kv = entering(own_kv, "seq", add_states, zero_state, False)
    suffix_qg = entering(own_qg, "seq", add_states, zero_state, True)
    causal_mask = jnp.arange(BLOCK)[:, None] >= jnp.arange(BLOCK)[None, :]
    state_before = prefix_kv
    state_after = suffix_qg + own_qg
    results = []
    for block_number in range(block_count):
        state_after = state_after - block_qg[block_number]
        results.append(
            block_outputs(
                query_blocks[block_number],
                key_blocks[block_number],
                value_blocks[block_number],
                grad_blocks[block_number],
                position[block_number * BLOCK : (block_number + 1) * BLOCK],
                state_before,
                state_after,
                causal_mask,
            )
        )
        state_before = state_before + block_kv[block_number]
    return tuple((jnp.concatenate([entry[slot] for entry in results], 0) for slot in range(4)))


def shards(queries, keys_in, values, cotangent):
    group_count = lax.axis_size("head")
    row_count, head_count, head_width = queries.shape
    grouped_shape = (row_count, group_count, head_count // group_count, head_width)
    grouped = (
        queries.reshape(grouped_shape),
        keys_in.reshape(grouped_shape),
        values.reshape(grouped_shape),
        cotangent.reshape(grouped_shape),
    )
    return local_work(
        (
            lax.all_to_all(grouped[0], "head", split_axis=1, concat_axis=0, tiled=True),
            lax.all_to_all(grouped[1], "head", split_axis=1, concat_axis=0, tiled=True),
            lax.all_to_all(grouped[2], "head", split_axis=1, concat_axis=0, tiled=True),
            lax.all_to_all(grouped[3], "head", split_axis=1, concat_axis=0, tiled=True),
        )
    )


def solution(mesh):
    in_specs = (
        P(("seq", "head"), None, None),
        P(("seq", "head"), None, None),
        P(("seq", "head"), None, None),
        P(("seq", "head"), None, None),
    )
    out_specs = (
        P("seq", "head", None),
        P("seq", "head", None),
        P("seq", "head", None),
        P("seq", "head", None),
    )
    return jax.shard_map(shards, mesh=mesh, in_specs=in_specs, out_specs=out_specs, check_vma=False)
```

profile of v0, /device:TPU:7, one launch (start us, length us, event | category | flops | bytes accessed | tf_op | source)
XLA Modules:
  0.0 284.7 jit_solution(9773119076046384603)
XLA Ops:
  7.2 2.7 copy.95
  9.9 8.2 %all-to-all-start = ((bf16[128,8,4,128]{3,0,2,1:T(8,128)(2,1)}), bf16[128,8,4,128]{3,0,2,1:T(8,128)(2,1)S(1)}, u32[]{:S(2)}, u32[]{:S(2)}) async-start(bf16[128,8,4,128]{3,0,2,1:T(8,128)(2,1)} %bitcast), calls=%async_computation | async-start | bytes 2097152 | tf_op jit(solution)/shard_map/all_to_all | solution.py:136
  18.1 1.4 copy.97
  19.4 27.8 %all-to-all-done = bf16[128,8,4,128]{3,0,2,1:T(8,128)(2,1)S(1)} async-done(((bf16[128,8,4,128]{3,0,2,1:T(8,128)(2,1)}), bf16[128,8,4,128]{3,0,2,1:T(8,128)(2,1)S(1)}, u32[]{:S(2)}, u32[]{:S(2)}) %all-to-all-start) | async-done | bytes 1048608 | tf_op jit(solution)/shard_map/all_to_all | solution.py:136
  47.2 3.6 %all-to-all-start.1 = ((bf16[128,8,4,128]{3,0,2,1:T(8,128)(2,1)}), bf16[128,8,4,128]{3,0,2,1:T(8,128)(2,1)S(1)}, u32[]{:S(2)}, u32[]{:S(2)}) async-start(bf16[128,8,4,128]{3,0,2,1:T(8,128)(2,1)} %bitcast.167), calls=%async_computation.1 | async-start | bytes 2097152 | tf_op jit(solution)/shard_map/all_to_all | solution.py:137
  50.9 1.0 copy.96
  51.9 28.1 %all-to-all-done.1 = bf16[128,8,4,128]{3,0,2,1:T(8,128)(2,1)S(1)} async-done(((bf16[128,8,4,128]{3,0,2,1:T(8,128)(2,1)}), bf16[128,8,4,128]{3,0,2,1:T(8,128)(2,1)S(1)}, u32[]{:S(2)}, u32[]{:S(2)}) %all-to-all-start.1) | async-done | bytes 1048608 | tf_op jit(solution)/shard_map/all_to_all | solution.py:137
  80.0 1.1 copy-done.21
  81.2 2.0 fusion.45
  83.2 2.6 copy.101
  85.8 4.2 %all-to-all-start.2 = ((bf16[128,8,4,128]{3,0,2,1:T(8,128)(2,1)}), bf16[128,8,4,128]{3,0,2,1:T(8,128)(2,1)}, u32[]{:S(2)}, u32[]{:S(2)}) async-start(bf16[128,8,4,128]{3,0,2,1:T(8,128)(2,1)} %bitcast.168), calls=%async_computation.2 | async-start | bytes 2097152 | tf_op jit(solution)/shard_map/all_to_all | solution.py:135
  90.0 2.6 copy.112
  92.6 26.6 %all-to-all-done.2 = bf16[128,8,4,128]{3,0,2,1:T(8,128)(2,1)} async-done(((bf16[128,8,4,128]{3,0,2,1:T(8,128)(2,1)}), bf16[128,8,4,128]{3,0,2,1:T(8,128)(2,1)}, u32[]{:S(2)}, u32[]{:S(2)}) %all-to-all-start.2) | async-done | bytes 1048608 | tf_op jit(solution)/shard_map/all_to_all | solution.py:135
  119.3 4.2 %all-to-all-start.3 = ((bf16[128,8,4,128]{3,0,2,1:T(8,128)(2,1)}), bf16[128,8,4,128]{3,0,2,1:T(8,128)(2,1)}, u32[]{:S(2)}, u32[]{:S(2)}) async-start(bf16[128,8,4,128]{3,0,2,1:T(8,128)(2,1)} %bitcast.166), calls=%async_computation.3 | async-start | bytes 2097152 | tf_op jit(solution)/shard_map/all_to_all | solution.py:138
  124.4 2.3 copy.117
  126.7 1.3 fusion.43
  132.4 20.3 %all-to-all-done.3 = bf16[128,8,4,128]{3,0,2,1:T(8,128)(2,1)} async-done(((bf16[128,8,4,128]{3,0,2,1:T(8,128)(2,1)}), bf16[128,8,4,128]{3,0,2,1:T(8,128)(2,1)}, u32[]{:S(2)}, u32[]{:S(2)}) %all-to-all-start.3) | async-done | bytes 1048608 | tf_op jit(solution)/shard_map/all_to_all | solution.py:138
  152.7 1.5 convert_bitcast_fusion
  154.5 1.1 copy-done.20
  155.6 1.6 fusion.46
  157.9 1.8 divide_convert_fusion.1
  159.8 1.8 select_convert_fusion.1
  163.5 2.1 select_convert_fusion.3
  165.7 1.5 convolution_bitcast_fusion.1
  167.2 1.8 convolution_bitcast_fusion.3
  169.0 1.5 convolution_bitcast_fusion
  170.4 1.8 convolution_bitcast_fusion.2
  172.2 1.8 convolution_bitcast_fusion.4
  174.0 1.5 fusion.23
  175.5 3.2 %fusion.27 = f32[4,128,512]{2,1,0:T(8,128)} fusion(bf16[4,512,512]{2,1,0:T(8,128)(2,1)} %select_convert_fusion.3, bf16[1024,4,128]{2,0,1:T(8,128)(2,1)S(1)} %divide_convert_fusion.1), kind=kOutput, calls=%fused_computation.56 | convolution fusion | flops 268435456 | bytes 3670016 | tf_op jit(solution)/shard_map/hts,the->she/dot_general | solution.py:62
  178.7 1.8 convolution_bitcast_fusion.5
  180.5 33.9 %while.30 = (s32[]{:T(128)}, f32[4,128,128]{2,1,0:T(8,128)S(1)}, s32[]{:T(128)}, bf16[32,4,128,128]{3,2,1,0:T(8,128)(2,1)}, s32[]{:T(128)}, /*index=5*/s32[]{:T(128)}) while((s32[]{:T(128)}, f32[4,128,128]{2,1,0:T(8,128)S(1)}, s32[]{:T(128)}, bf16[32,4,128,128]{3,2,1,0:T(8,128)(2,1)}, s32[]{:T(128)}, /*index=5*/s32[]{:T(128)}) %tuple.96), condition=%wide.region_2.3_spmd.clone, body=%wide.region_1.0_spmd.clone.sunk | while | flops 262148 | bytes 655461 | solution.py:21
  182.7 1.0 add_select_fusion.4
  183.7 1.0 add_select_fusion.4
  184.8 1.0 add_select_fusion.4
  185.8 1.0 add_select_fusion.4
  186.9 1.0 add_select_fusion.4
  189.0 1.0 add_select_fusion.4
  190.1 1.0 add_select_fusion.4
  192.2 1.0 add_select_fusion.4
  193.3 1.0 add_select_fusion.4
  195.4 1.0 add_select_fusion.4
  196.5 1.0 add_select_fusion.4
  198.6 1.0 add_select_fusion.4
  199.6 1.0 add_select_fusion.4
  201.8 1.0 add_select_fusion.4
  202.8 1.0 add_select_fusion.4
  203.9 1.0 add_select_fusion.4
  204.9 1.0 add_select_fusion.4
  206.0 1.0 add_select_fusion.4
  207.1 1.0 add_select_fusion.4
  209.2 1.0 add_select_fusion.4
  212.4 1.0 add_select_fusion.4
  214.5 8.4 %all-gather.7.cloned.1.call-done = bf16[128,128,128]{2,1,0:T(8,128)(2,1)} async-done(((bf16[4,128,128]{2,1,0:T(8,128)(2,1)}), bf16[128,128,128]{2,1,0:T(8,128)(2,1)}) %all-gather.7.cloned.1.call-update) | async-done | bytes 4194320 | tf_op jit(solution)/shard_map/all_gather | solution.py:12
  222.9 34.1 %while.31 = (s32[]{:T(128)}, f32[4,128,128]{2,1,0:T(8,128)S(1)}, s32[]{:T(128)}, bf16[32,4,128,128]{3,2,1,0:T(8,128)(2,1)}, s32[]{:T(128)}, /*index=5*/s32[]{:T(128)}, s32[]{:T(128)}, s32[]{:T(128)}) while((s32[]{:T(128)}, f32[4,128,128]{2,1,0:T(8,128)S(1)}, s32[]{:T(128)}, bf16[32,4,128,128]{3,2,1,0:T(8,128)(2,1)}, s32[]{:T(128)}, ...), condition=%wide.region_5.6_spmd.clone, body=%wide.region_4.5_spmd.clone.sunk | while | flops 262152 | bytes 655523 | solution.py:21
  257.8 1.1 fusion.35
  258.9 2.3 fusion.10
  262.8 1.1 pad_maximum_fusion.2
  263.9 2.4 copy.132
  266.4 1.5 fusion.11
  267.9 1.1 pad_maximum_fusion.1
  269.0 2.4 copy.131
  273.1 1.4 copy.133
  276.4 1.4 copy.130
  (124 shorter events, 58.9 us)
Async XLA Ops:
  7.2 10.9 %copy-start.19 = (bf16[128,32,128]{2,1,0:T(8,128)(2,1)S(1)}, bf16[128,32,128]{2,1,0:T(8,128)(2,1)}, u32[]{:S(2)}) copy-start(bf16[128,32,128]{2,1,0:T(8,128)(2,1)} %param.10) | copy-start | bytes 3145732
  9.9 37.4 %all-to-all-start = ((bf16[128,8,4,128]{3,0,2,1:T(8,128)(2,1)}), bf16[128,8,4,128]{3,0,2,1:T(8,128)(2,1)S(1)}, u32[]{:S(2)}, u32[]{:S(2)}) async-start(bf16[128,8,4,128]{3,0,2,1:T(8,128)(2,1)} %bitcast), calls=%async_computation | async-start | bytes 2097152 | tf_op jit(solution)/shard_map/all_to_all | solution.py:136
  47.2 32.7 %all-to-all-start.1 = ((bf16[128,8,4,128]{3,0,2,1:T(8,128)(2,1)}), bf16[128,8,4,128]{3,0,2,1:T(8,128)(2,1)S(1)}, u32[]{:S(2)}, u32[]{:S(2)}) async-start(bf16[128,8,4,128]{3,0,2,1:T(8,128)(2,1)} %bitcast.167), calls=%async_computation.1 | async-start | bytes 2097152 | tf_op jit(solution)/shard_map/all_to_all | solution.py:137
  50.8 129.7 %all-gather.5.cloned.1.call-start = ((), (), s32[]{:S(2)}) async-start(), calls=%async_computation.4 | async-start | bytes 4325376 | tf_op jit(solution)/shard_map/all_gather | solution.py:12
  80.0 1.2 copy-start.21
  85.8 33.5 %all-to-all-start.2 = ((bf16[128,8,4,128]{3,0,2,1:T(8,128)(2,1)}), bf16[128,8,4,128]{3,0,2,1:T(8,128)(2,1)}, u32[]{:S(2)}, u32[]{:S(2)}) async-start(bf16[128,8,4,128]{3,0,2,1:T(8,128)(2,1)} %bitcast.168), calls=%async_computation.2 | async-start | bytes 2097152 | tf_op jit(solution)/shard_map/all_to_all | solution.py:135
  119.3 33.5 %all-to-all-start.3 = ((bf16[128,8,4,128]{3,0,2,1:T(8,128)(2,1)}), bf16[128,8,4,128]{3,0,2,1:T(8,128)(2,1)}, u32[]{:S(2)}, u32[]{:S(2)}) async-start(bf16[128,8,4,128]{3,0,2,1:T(8,128)(2,1)} %bitcast.166), calls=%async_computation.3 | async-start | bytes 2097152 | tf_op jit(solution)/shard_map/all_to_all | solution.py:138
  123.5 99.4 %all-gather.7.cloned.1.call-start = ((), (), s32[]{:S(2)}) async-start(), calls=%async_computation.5 | async-start | bytes 4325376 | tf_op jit(solution)/shard_map/all_gather | solution.py:12
  154.2 1.4 copy-start.20
  154.4 2.7 copy-start.1
  157.1 2.7 copy-start.4
  159.8 1.8 copy-start.3
  159.8 1.8 copy-start.23
  161.6 1.0 copy-start.2
  161.6 1.2 copy-start.13
  162.4 1.2 copy-start.11
  175.5 3.2 %copy-start = (bf16[4,512,512]{2,1,0:T(8,128)(2,1)S(1)}, bf16[4,512,512]{2,1,0:T(8,128)(2,1)}, u32[]{:S(2)}) copy-start(bf16[4,512,512]{2,1,0:T(8,128)(2,1)} %select_convert_fusion.3) | copy-start | bytes 6291460
  175.5 3.2 %copy-start.5 = (bf16[4,128,1,4,128]{4,1,0,3,2:T(8,128)(2,1)S(1)}, bf16[4,128,1,4,128]{4,1,0,3,2:T(8,128)(2,1)}, u32[]{:S(2)}) copy-start(bf16[4,128,1,4,128]{4,1,0,3,2:T(8,128)(2,1)} %copy.105) | copy-start | bytes 1572868
  257.8 3.5 %copy-start.18 = (f32[4,128,128]{1,2,0:T(8,128)S(1)}, f32[4,128,128]{1,2,0:T(8,128)}, u32[]{:S(2)}) copy-start(f32[4,128,128]{1,2,0:T(8,128)} %copy.121) | copy-start | bytes 786436
  257.8 3.5 %copy-start.22 = (f32[2,4,128,128]{2,3,1,0:T(8,128)S(1)}, f32[2,4,128,128]{2,3,1,0:T(8,128)}, u32[]{:S(2)}) copy-start(f32[2,4,128,128]{2,3,1,0:T(8,128)} %get-tuple-element.282) | copy-start | bytes 1572868
  257.8 3.5 %copy-start.6 = (bf16[4,128,1,4,128]{4,1,0,3,2:T(8,128)(2,1)S(1)}, bf16[4,128,1,4,128]{4,1,0,3,2:T(8,128)(2,1)}, u32[]{:S(2)}) copy-start(bf16[4,128,1,4,128]{4,1,0,3,2:T(8,128)(2,1)} %copy.105) | copy-start | bytes 1572868
  257.8 3.6 %copy-start.10 = (f32[512,4,128]{0,2,1:T(8,128)S(1)}, f32[512,4,128]{0,2,1:T(8,128)}, u32[]{:S(2)}) copy-start(f32[512,4,128]{0,2,1:T(8,128)} %convolution_bitcast_fusion.1) | copy-start | bytes 3145732
  261.3 1.2 copy-start.9
  263.9 4.0 %copy-start.15 = (bf16[512,4,128]{0,2,1:T(8,128)(2,1)S(1)}, bf16[512,4,128]{0,2,1:T(8,128)(2,1)}, u32[]{:S(2)}) copy-start(bf16[512,4,128]{0,2,1:T(8,128)(2,1)} %fusion.10) | copy-start | bytes 1572868
  267.9 3.5 %copy-start.7 = (f32[4,128,512]{2,1,0:T(8,128)S(1)}, f32[4,128,512]{2,1,0:T(8,128)}, u32[]{:S(2)}) copy-start(f32[4,128,512]{2,1,0:T(8,128)} %fusion.23) | copy-start | bytes 3145732
  271.4 1.2 copy-start.8
  273.0 1.6 copy-start.14
  273.0 1.6 copy-start.16
  274.6 1.0 copy-start.12
  274.6 1.4 copy-start.17
Sparse Core Ops, SparseCore 0:
  83.3 47.1 all-gather.4
  175.6 47.2 all-gather.6
where the time goes:
time: 288 us; the launch traced here: 285 us
  waiting for transfers between devices  111 us (39%)
  other arithmetic  74.2 us (26%)
  local copies, waits for them, and re-layouts  33.4 us (12%)
  matrix products  29.5 us (10%)
  starting transfers between devices  20.3 us (7%)
  between operations  14.5 us (5%)
    select_n x64, other arithmetic, step(): return jnp.where(reached, new, before)  66.4 us
    all_to_all x1, waiting for transfers between devices, shards(): lax.all_to_all(grouped[2], 'head', split_axis=1, concat_axis=0, tiled=True)  28.1 us
    all_to_all x1, waiting for transfers between devices, shards(): lax.all_to_all(grouped[1], 'head', split_axis=1, concat_axis=0, tiled=True)  27.8 us
    all_to_all x1, waiting for transfers between devices, shards(): lax.all_to_all(grouped[0], 'head', split_axis=1, concat_axis=0, tiled=True)  26.6 us
    unnamed x56, local copies, waits for them, and re-layouts  22.5 us
    all_to_all x1, waiting for transfers between devices, shards(): lax.all_to_all(grouped[3], 'head', split_axis=1, concat_axis=0, tiled=True)  20.3 us
    all_gather x2, waiting for transfers between devices, entering(): everything = lax.all_gather(x.astype(jnp.bfloat16), axis)  8.4 us
    all_to_all x1, starting transfers between devices, shards(): lax.all_to_all(grouped[1], 'head', split_axis=1, concat_axis=0, tiled=True)  8.19 us
  transfers between devices with their start and end apart: 6, of which 5 were waited for; matrix products, arithmetic and copies ran while one was open for 27% of the time, Pallas kernels for 0%

commit v1 on v0

v1 whole, which is shorter than its diff:
```python
import functools

import jax
import jax.numpy as jnp
from jax import lax
from jax.experimental import pallas as pl
from jax.experimental.pallas import tpu as pltpu
from jax.sharding import PartitionSpec as P

BLOCK = 512
OFFSET = 1048576
MESH = pl.DeviceIdType.MESH
NZ = 8
NX = 4
NY = 4
ROWS = 128
HALF = 64
FAR_FIRST = (4, 3, 5, 2, 6, 1, 7)
F32 = jnp.float32
BF16 = jnp.bfloat16


def dot(a, b, dims):
    return lax.dot_general(a, b, (dims, ((), ())), preferred_element_type=F32)


NN = ((1,), (0,))
NT = ((1,), (1,))
TN = ((0,), (0,))


def exchange_kernel(
    q_ref, k_ref, v_ref, g_ref, rows_out, states_out,
    inb, stg, sbuf, rbuf, recip, own, csend, cbuf, ysend, ybuf, xsend, xbuf, fsend, fbuf, stout,
    in_sem, s0_sem, r0_sem, s_sem, r_sem, l_sem, o_sem, st_sem,
    cs_sem, cr_sem, ys_sem, yr_sem, xs_sem, xr_sem, fs_sem, fr_sem,
):
    z = lax.axis_index("head")
    seq = lax.axis_index("seq")
    core = lax.rem(seq, 2)
    chip = seq // 2
    y = lax.rem(chip, NY)
    x = chip // NY
    partner = seq + 1 - 2 * core

    def y_peer(d):
        return (x * NY + lax.rem(y + d, NY)) * 2 + core

    def x_peer(d):
        return (lax.rem(x + d, NX) * NY + y) * 2 + core

    loads = []
    for a, ref in enumerate((k_ref, v_ref, q_ref, g_ref)):
        copy = pltpu.make_async_copy(ref, inb.at[a], in_sem.at[a])
        copy.start()
        loads.append(copy)

    barrier = pltpu.get_barrier_semaphore()
    for d in range(1, NZ):
        pl.semaphore_signal(
            barrier, inc=1, device_id={"head": lax.rem(z + d, NZ)}, device_id_type=MESH
        )
    for peer in [y_peer(d) for d in (1, 2, 3)] + [x_peer(d) for d in (1, 2, 3)] + [partner]:
        pl.semaphore_signal(barrier, inc=1, device_id={"seq": peer}, device_id_type=MESH)

    first_row = (seq * NZ + z) * ROWS + OFFSET + 1
    position = (first_row + lax.broadcasted_iota(jnp.int32, (ROWS, 128), 0)).astype(F32)
    recip[...] = 1.0 / position

    def head_major(hl, a):
        for dest in range(NZ):
            part = stg[a, pl.ds(dest * 4 + hl, ROWS, stride=32), :]
            if a == 3:
                part = part * recip[...]
            sbuf[hl, dest, a] = part.astype(BF16)

    def first_copy(a, d):
        dest = lax.rem(z + d, NZ)
        return pltpu.make_async_remote_copy(
            src_ref=sbuf.at[0, dest, a],
            dst_ref=rbuf.at[0, a, pl.ds(pl.multiple_of(z * ROWS, ROWS), ROWS), :],
            send_sem=s0_sem.at[a, d],
            recv_sem=r0_sem.at[a, d],
            device_id={"head": dest},
            device_id_type=MESH,
        )

    def stage_copy(hl, d):
        dest = lax.rem(z + d, NZ)
        return pltpu.make_async_remote_copy(
            src_ref=sbuf.at[hl, dest],
            dst_ref=rbuf.at[hl, :, pl.ds(pl.multiple_of(z * ROWS, ROWS), ROWS), :],
            send_sem=s_sem.at[hl, d],
            recv_sem=r_sem.at[hl, d],
            device_id={"head": dest},
            device_id_type=MESH,
        )

    def local_copy(hl):
        return pltpu.make_async_copy(
            sbuf.at[hl, z],
            rbuf.at[hl, :, pl.ds(pl.multiple_of(z * ROWS, ROWS), ROWS), :],
            l_sem.at[hl],
        )

    for a in range(4):
        loads[a].wait()
        stg[a] = inb[a].astype(F32)
        head_major(0, a)
        if a == 0:
            pl.semaphore_wait(barrier, 14)
        for d in FAR_FIRST:
            first_copy(a, d).start()
    local_copy(0).start()
    for hl in range(1, 4):
        for a in range(4):
            head_major(hl, a)
        for d in FAR_FIRST:
            stage_copy(hl, d).start()
        local_copy(hl).start()

    def c_copy(hl):
        return pltpu.make_async_remote_copy(
            src_ref=csend.at[hl], dst_ref=cbuf.at[hl],
            send_sem=cs_sem.at[hl], recv_sem=cr_sem.at[hl],
            device_id={"seq": partner}, device_id_type=MESH,
        )

    def y_copy(hl, d):
        return pltpu.make_async_remote_copy(
            src_ref=ysend.at[hl], dst_ref=ybuf.at[hl, y],
            send_sem=ys_sem.at[hl, d], recv_sem=yr_sem.at[hl, d],
            device_id={"seq": y_peer(d)}, device_id_type=MESH,
        )

    def x_copy(hl, d):
        later = (lax.rem(x + d, NX) > x).astype(jnp.int32)
        return pltpu.make_async_remote_copy(
            src_ref=xsend.at[hl, 1 - later], dst_ref=xbuf.at[hl, x],
            send_sem=xs_sem.at[hl, d], recv_sem=xr_sem.at[hl, d],
            device_id={"seq": x_peer(d)}, device_id_type=MESH,
        )

    def f_copy(hl):
        return pltpu.make_async_remote_copy(
            src_ref=fsend.at[hl], dst_ref=fbuf.at[hl],
            send_sem=fs_sem.at[hl], recv_sem=fr_sem.at[hl],
            device_id={"seq": partner}, device_id_type=MESH,
        )

    mine = pl.ds(pl.multiple_of(core * HALF, HALF), HALF)
    other = pl.ds(pl.multiple_of((1 - core) * HALF, HALF), HALF)
    outs = []
    for hl in range(4):
        if hl == 0:
            for a in range(4):
                for d in FAR_FIRST:
                    first_copy(a, d).wait_recv()
        else:
            for d in FAR_FIRST:
                stage_copy(hl, d).wait_recv()
        local_copy(hl).wait()
        out = pltpu.make_async_copy(rbuf.at[hl], rows_out.at[hl], o_sem.at[hl])
        out.start()
        outs.append(out)
        for b in range(2):
            rows = pl.ds(b * BLOCK, BLOCK)
            own[b] = dot(rbuf[hl, 0, rows, :], rbuf[hl, 1, rows, :], TN)
            own[2 + b] = dot(rbuf[hl, 2, rows, :], rbuf[hl, 3, rows, :], TN)
        csend[hl, 0] = (own[0, other, :] + own[1, other, :]).astype(BF16)
        csend[hl, 1] = (own[2, other, :] + own[3, other, :]).astype(BF16)
        c_copy(hl).start()
        own_kv = own[0, mine, :] + own[1, mine, :]
        own_qg = own[2, mine, :] + own[3, mine, :]
        c_copy(hl).wait_recv()
        pair_kv = cbuf[hl, 0].astype(F32)
        pair_qg = cbuf[hl, 1].astype(F32)
        chip_kv = own_kv + pair_kv
        chip_qg = own_qg + pair_qg
        ysend[hl, 0] = chip_kv.astype(BF16)
        ysend[hl, 1] = chip_qg.astype(BF16)
        for d in (2, 1, 3):
            y_copy(hl, d).start()
        for d in (1, 3, 2):
            y_copy(hl, d).wait_recv()
        row_kv = chip_kv
        row_qg = chip_qg
        before = jnp.zeros((HALF, 128), F32)
        after = jnp.zeros((HALF, 128), F32)
        for d in (1, 2, 3):
            source = lax.rem(y + d, NY)
            got_kv = ybuf[hl, source, 0].astype(F32)
            got_qg = ybuf[hl, source, 1].astype(F32)
            row_kv = row_kv + got_kv
            row_qg = row_qg + got_qg
            before = before + jnp.where(source < y, got_kv, 0.0)
            after = after + jnp.where(source > y, got_qg, 0.0)
        xsend[hl, 0] = row_kv.astype(BF16)
        xsend[hl, 1] = row_qg.astype(BF16)
        for d in (2, 1, 3):
            x_copy(hl, d).start()
        for d in (1, 3, 2):
            x_copy(hl, d).wait_recv()
        for d in (1, 2, 3):
            source = lax.rem(x + d, NX)
            got = xbuf[hl, source].astype(F32)
            before = before + jnp.where(source < x, got, 0.0)
            after = after + jnp.where(source > x, got, 0.0)
        fsend[hl, 0] = (before + jnp.where(core == 0, own_kv, 0.0)).astype(BF16)
        fsend[hl, 1] = (after + jnp.where(core == 1, own_qg, 0.0)).astype(BF16)
        f_copy(hl).start()
        before = before + jnp.where(core == 1, pair_kv, 0.0)
        after = after + jnp.where(core == 0, pair_qg, 0.0)
        stout[hl, 0, mine, :] = before.astype(BF16)
        stout[hl, 1, mine, :] = (before + own[0, mine, :]).astype(BF16)
        stout[hl, 2, mine, :] = (after + own[3, mine, :]).astype(BF16)
        stout[hl, 3, mine, :] = after.astype(BF16)
        f_copy(hl).wait_recv()
        before = fbuf[hl, 0].astype(F32)
        after = fbuf[hl, 1].astype(F32)
        stout[hl, 0, other, :] = before.astype(BF16)
        stout[hl, 1, other, :] = (before + own[0, other, :]).astype(BF16)
        stout[hl, 2, other, :] = (after + own[3, other, :]).astype(BF16)
        stout[hl, 3, other, :] = after.astype(BF16)
        out = pltpu.make_async_copy(stout.at[hl], states_out.at[hl], st_sem.at[hl])
        out.start()
        outs.append(out)
    for hl in range(4):
        for d in FAR_FIRST:
            if hl == 0:
                for a in range(4):
                    first_copy(a, d).wait_send()
            else:
                stage_copy(hl, d).wait_send()
        c_copy(hl).wait_send()
        f_copy(hl).wait_send()
        for d in (1, 2, 3):
            y_copy(hl, d).wait_send()
            x_copy(hl, d).wait_send()
    for out in outs:
        out.wait()


def exchange(queries, keys_in, values, cotangent):
    flat = [a.reshape(ROWS * 32, 128) for a in (queries, keys_in, values, cotangent)]
    any_space = pl.BlockSpec(memory_space=pl.ANY)
    dma = pltpu.SemaphoreType.DMA
    return pl.pallas_call(
        exchange_kernel,
        out_shape=(
            jax.ShapeDtypeStruct((4, 4, 1024, 128), BF16),
            jax.ShapeDtypeStruct((4, 4, 128, 128), BF16),
        ),
        in_specs=[any_space] * 4,
        out_specs=(any_space, any_space),
        scratch_shapes=[
            pltpu.VMEM((4, ROWS * 32, 128), BF16),
            pltpu.VMEM((4, ROWS * 32, 128), F32),
            pltpu.VMEM((4, NZ, 4, ROWS, 128), BF16),
            pltpu.VMEM((4, 4, 1024, 128), BF16),
            pltpu.VMEM((ROWS, 128), F32),
            pltpu.VMEM((4, 128, 128), F32),
            pltpu.VMEM((4, 2, HALF, 128), BF16),
            pltpu.VMEM((4, 2, HALF, 128), BF16),
            pltpu.VMEM((4, 2, HALF, 128), BF16),
            pltpu.VMEM((4, NY, 2, HALF, 128), BF16),
            pltpu.VMEM((4, 2, HALF, 128), BF16),
            pltpu.VMEM((4, NX, HALF, 128), BF16),
            pltpu.VMEM((4, 2, HALF, 128), BF16),
            pltpu.VMEM((4, 2, HALF, 128), BF16),
            pltpu.VMEM((4, 4, 128, 128), BF16),
            dma((4,)), dma((4, NZ)), dma((4, NZ)), dma((4, NZ)), dma((4, NZ)),
            dma((4,)), dma((4,)), dma((4,)),
            dma((4,)), dma((4,)), dma((4, 4)), dma((4, 4)), dma((4, 4)), dma((4, 4)),
            dma((4,)), dma((4,)),
        ],
        compiler_params=pltpu.CompilerParams(
            collective_id=0, has_side_effects=True, vmem_limit_bytes=63 << 20
        ),
        name="exchange",
    )(*flat)


def blocks_kernel(rows_ref, states_ref, att_ref, gq_ref, gk_ref, gv_ref, acc):
    b = pl.program_id(0)
    h = pl.program_id(1)
    seq = lax.axis_index("seq")
    k, v, q, g = (rows_ref[0, a] for a in range(4))
    before = states_ref[0, b]
    after = states_ref[0, 2 + b]
    mask = lax.broadcasted_iota(jnp.int32, (BLOCK, BLOCK), 0) >= lax.broadcasted_iota(
        jnp.int32, (BLOCK, BLOCK), 1
    )
    score = jnp.where(mask, dot(q, k, NT), 0.0).astype(BF16)
    grad_score = jnp.where(mask, dot(g, v, NT), 0.0).astype(BF16)
    position = (
        seq * 1024 + b * BLOCK + OFFSET + 1
        + lax.broadcasted_iota(jnp.int32, (BLOCK, 128), 0)
    ).astype(F32)
    mine = pl.ds(h, BLOCK, stride=4)
    acc[0, mine, :] = (dot(q, before, NN) + dot(score, v, NN)) / position
    acc[1, mine, :] = dot(g, before, NT) + dot(grad_score, k, NN)
    acc[2, mine, :] = dot(v, after, NT) + dot(grad_score, q, TN)
    acc[3, mine, :] = dot(k, after, NN) + dot(score, g, TN)

    @pl.when(h == 3)
    def _():
        att_ref[...] = acc[0].astype(BF16)
        gq_ref[...] = acc[1].astype(BF16)
        gk_ref[...] = acc[2].astype(BF16)
        gv_ref[...] = acc[3].astype(BF16)


def block_outputs(rows, states):
    out = jax.ShapeDtypeStruct((4096, 128), BF16)
    out_spec = pl.BlockSpec((BLOCK * 4, 128), lambda b, h: (b, 0))
    results = pl.pallas_call(
        blocks_kernel,
        out_shape=(out,) * 4,
        grid=(2, 4),
        in_specs=[
            pl.BlockSpec((1, 4, BLOCK, 128), lambda b, h: (h, 0, b, 0)),
            pl.BlockSpec((1, 4, 128, 128), lambda b, h: (h, 0, 0, 0)),
        ],
        out_specs=(out_spec,) * 4,
        scratch_shapes=[pltpu.VMEM((4, BLOCK * 4, 128), F32)],
        compiler_params=pltpu.CompilerParams(vmem_limit_bytes=40 << 20),
        name="blocks",
    )(rows, states)
    return tuple(r.reshape(1024, 4, 128) for r in results)


def shards(queries, keys_in, values, cotangent):
    rows, states = exchange(queries, keys_in, values, cotangent)
    return block_outputs(rows, states)


def solution(mesh):
    in_specs = (P(("seq", "head"), None, None),) * 4
    out_specs = (P("seq", "head", None),) * 4
    return jax.shard_map(shards, mesh=mesh, in_specs=in_specs, out_specs=out_specs, check_vma=False)
```

time: 288 us -> 130 us (0.45)
  Pallas kernels: 0 us -> 124 us
  waiting for transfers between devices: 111 us -> 0 us
  other arithmetic: 74.2 us -> 0 us
  local copies, waits for them, and re-layouts: 33.4 us -> 3.22 us
  matrix products: 29.5 us -> 0 us
  starting transfers between devices: 20.3 us -> 0 us
  between operations: 14.5 us -> 0.65 us
    pallas_call x0 -> x2, Pallas kernels: none -> 124 us  [the longest x1 112 us: exchange(): pl.pallas_call(exchange_kernel, out_shape=(jax.ShapeDtypeStruct((4, 4, 10...]
    all_to_all x4 -> x0, waiting for transfers between devices: 103 us -> none  [the longest x1 28.1 us: shards(): lax.all_to_all(grouped[2], 'head', split_axis=1, concat_axis=0, tiled=True)]
    select_n x64 -> x0, other arithmetic: 66.4 us -> none  [step(): return jnp.where(reached, new, before)]
    dot_general x22 -> x0, matrix products: 29.5 us -> none  [the longest x4 5.38 us: masked_scores(): jnp.einsum('thd,shd->hts', left_side, right_side, preferred_element_type=...]
    all_to_all x4 -> x0, starting transfers between devices: 20.2 us -> none  [the longest x1 8.19 us: shards(): lax.all_to_all(grouped[1], 'head', split_axis=1, concat_axis=0, tiled=True)]
    unnamed x56 -> x4, local copies, waits for them, and re-layouts: 22.5 us -> 3.22 us
    all_gather x2 -> x0, waiting for transfers between devices: 8.4 us -> none  [entering(): everything = lax.all_gather(x.astype(jnp.bfloat16), axis)]
    slice x10 -> x0, local copies, waits for them, and re-layouts: 5.68 us -> none  [the longest x3 2.92 us: local_work(): query_blocks[block_number]]
  transfers between devices with their start and end apart: 6 -> 0, of which waited for: 5 -> 0; matrix products, arithmetic and copies ran while one was open for 27% -> 0% of each run, Pallas kernels for 0% -> 0%
where the time goes in v1:
time: 130 us; the launch traced here: 127 us
  Pallas kernels  124 us (95%)
  local copies, waits for them, and re-layouts  3.22 us (2%)
    pallas_call x1, Pallas kernels, exchange(): pl.pallas_call(exchange_kernel, out_shape=(jax.ShapeDtypeStruct((4, 4, 10...  112 us
    pallas_call x1, Pallas kernels, block_outputs(): pl.pallas_call(blocks_kernel, out_shape=(out,) * 4, grid=(2, 4), in_specs...  11.3 us
    unnamed x4, local copies, waits for them, and re-layouts  3.22 us

profile of v1, /device:TPU:7, one launch (start us, length us, event | category | flops | bytes accessed | tf_op | source)
XLA Modules:
  0.0 127.5 jit_solution(371744631694671906)
XLA Ops:
  0.6 112.3 %exchange.1 = (bf16[4,4,1024,128]{3,2,1,0:T(8,128)(2,1)}, bf16[4,4,128,128]{3,2,1,0:T(8,128)(2,1)}) custom-call(bf16[4096,128]{1,0:T(8,128)(2,1)} %bitcast.8, bf16[4096,128]{1,0:T(8,128)(2,1)} %bitcast.9, bf16[4096,128]{1,0:T(8,128)(2,1)} %bitcast.10, bf16[4096,128]{1,0:T(8,128)(2,1)} %bitcast.11), custom_call_target="tpu_custom_call" | custom-call | tf_op jit(solution)/shard_map/exchange/pallas_call | solution.py:248
  112.9 0.0 copy-start
  112.9 2.2 %copy-done = bf16[4,4,1024,128]{3,2,1,0:T(8,128)(2,1)S(1)} copy-done((bf16[4,4,1024,128]{3,2,1,0:T(8,128)(2,1)S(1)}, bf16[4,4,1024,128]{3,2,1,0:T(8,128)(2,1)}, u32[]{:S(2)}) %copy-start) | copy-done | bytes 4194328
  115.1 0.0 copy-start.1
  115.1 1.0 copy-done.1
  116.2 11.3 %blocks.1 = (bf16[4096,128]{1,0:T(8,128)(2,1)}, bf16[4096,128]{1,0:T(8,128)(2,1)}, bf16[4096,128]{1,0:T(8,128)(2,1)}, bf16[4096,128]{1,0:T(8,128)(2,1)}) custom-call(bf16[4,4,1024,128]{3,2,1,0:T(8,128)(2,1)S(1)} %copy-done, bf16[4,4,128,128]{3,2,1,0:T(8,128)(2,1)S(1)} %copy-done.1), custom_call_target="tpu_custom_call" | custom-call | tf_op jit(solution)/shard_map/blocks/pallas_call | solution.py:317
Async XLA Ops:
  112.9 2.2 %copy-start = (bf16[4,4,1024,128]{3,2,1,0:T(8,128)(2,1)S(1)}, bf16[4,4,1024,128]{3,2,1,0:T(8,128)(2,1)}, u32[]{:S(2)}) copy-start(bf16[4,4,1024,128]{3,2,1,0:T(8,128)(2,1)} %get-tuple-element.10.rows_ref) | copy-start | bytes 12582916
  115.1 1.0 copy-start.1

commit v2 on v1

v2 whole, which is shorter than its diff:
```python
import functools

import jax
import jax.numpy as jnp
from jax import lax
from jax.experimental import pallas as pl
from jax.experimental.pallas import tpu as pltpu
from jax.sharding import PartitionSpec as P

BLOCK = 512
OFFSET = 1048576
MESH = pl.DeviceIdType.MESH
NZ = 8
NX = 4
NY = 4
ROWS = 128
HALF = 64
STRIP = 256
FAR_FIRST = (4, 3, 5, 2, 6, 1, 7)
F32 = jnp.float32
BF16 = jnp.bfloat16


def dot(a, b, dims):
    return lax.dot_general(a, b, (dims, ((), ())), preferred_element_type=F32)


NN = ((1,), (0,))
NT = ((1,), (1,))
TN = ((0,), (0,))


def exchange_kernel(
    q_ref, k_ref, v_ref, g_ref, out_ref,
    inb, stg, sbuf, rbuf, recip, recip_out, own, part, before_used, after_used,
    csend, cbuf, ysend, ybuf, xsend, xbuf, fsend, fbuf,
    in_sem, s_sem, r_sem, l_sem,
    cs_sem, cr_sem, ys_sem, yr_sem, xs_sem, xr_sem, fs_sem, fr_sem,
):
    z = lax.axis_index("head")
    seq = lax.axis_index("seq")
    core = lax.rem(seq, 2)
    chip = seq // 2
    y = lax.rem(chip, NY)
    x = chip // NY
    partner = seq + 1 - 2 * core

    def y_peer(d):
        return (x * NY + lax.rem(y + d, NY)) * 2 + core

    def x_peer(d):
        return (lax.rem(x + d, NX) * NY + y) * 2 + core

    loads = []
    for a, ref in enumerate((k_ref, v_ref, q_ref, g_ref)):
        copy = pltpu.make_async_copy(ref, inb.at[a], in_sem.at[a])
        copy.start()
        loads.append(copy)

    barrier = pltpu.get_barrier_semaphore()
    for d in range(1, NZ):
        pl.semaphore_signal(
            barrier, inc=1, device_id={"head": lax.rem(z + d, NZ)}, device_id_type=MESH
        )
    for peer in [y_peer(d) for d in (1, 2, 3)] + [x_peer(d) for d in (1, 2, 3)] + [partner]:
        pl.semaphore_signal(barrier, inc=1, device_id={"seq": peer}, device_id_type=MESH)

    first_row = (seq * NZ + z) * ROWS + OFFSET + 1
    position = (first_row + lax.broadcasted_iota(jnp.int32, (ROWS, 128), 0)).astype(F32)
    recip[...] = 1.0 / position

    def head_major(hl, a):
        for dest in range(NZ):
            piece = stg[a, pl.ds(dest * 4 + hl, ROWS, stride=32), :]
            if a == 3:
                piece = piece * recip[...]
            sbuf[hl, dest, a] = piece.astype(BF16)

    here = pl.ds(pl.multiple_of(z * ROWS, ROWS), ROWS)

    def z_copy(hl, a, d):
        dest = lax.rem(z + d, NZ)
        return pltpu.make_async_remote_copy(
            src_ref=sbuf.at[hl, dest, a],
            dst_ref=rbuf.at[hl, a, here, :],
            send_sem=s_sem.at[hl, a, d],
            recv_sem=r_sem.at[hl, a, d],
            device_id={"head": dest},
            device_id_type=MESH,
        )

    def local_copy(hl):
        return pltpu.make_async_copy(sbuf.at[hl, z], rbuf.at[hl, :, here, :], l_sem.at[hl])

    for a in range(4):
        loads[a].wait()
        stg[a] = inb[a].astype(F32)
        head_major(0, a)
        if a == 0:
            pl.semaphore_wait(barrier, 14)
        for d in FAR_FIRST:
            z_copy(0, a, d).start()
    local_copy(0).start()
    for hl in range(1, 4):
        for a in range(4):
            head_major(hl, a)
            for d in FAR_FIRST:
                z_copy(hl, a, d).start()
        local_copy(hl).start()

    position = (
        seq * 1024 + OFFSET + 1 + lax.broadcasted_iota(jnp.int32, (1024, 128), 0)
    ).astype(F32)
    recip_out[...] = 1.0 / position

    def c_copy(hl):
        return pltpu.make_async_remote_copy(
            src_ref=csend.at[hl], dst_ref=cbuf.at[hl],
            send_sem=cs_sem.at[hl], recv_sem=cr_sem.at[hl],
            device_id={"seq": partner}, device_id_type=MESH,
        )

    def y_copy(hl, d):
        return pltpu.make_async_remote_copy(
            src_ref=ysend.at[hl], dst_ref=ybuf.at[hl, y],
            send_sem=ys_sem.at[hl, d], recv_sem=yr_sem.at[hl, d],
            device_id={"seq": y_peer(d)}, device_id_type=MESH,
        )

    def x_copy(hl, d):
        later = (lax.rem(x + d, NX) > x).astype(jnp.int32)
        return pltpu.make_async_remote_copy(
            src_ref=xsend.at[hl, 1 - later], dst_ref=xbuf.at[hl, x],
            send_sem=xs_sem.at[hl, d], recv_sem=xr_sem.at[hl, d],
            device_id={"seq": x_peer(d)}, device_id_type=MESH,
        )

    def f_copy(hl):
        return pltpu.make_async_remote_copy(
            src_ref=fsend.at[hl], dst_ref=fbuf.at[hl],
            send_sem=fs_sem.at[hl], recv_sem=fr_sem.at[hl],
            device_id={"seq": partner}, device_id_type=MESH,
        )

    mine = pl.ds(pl.multiple_of(core * HALF, HALF), HALF)
    other = pl.ds(pl.multiple_of((1 - core) * HALF, HALF), HALF)

    def within_block(hl, b):
        for t in range(2):
            rows = pl.ds(b * BLOCK + t * STRIP, STRIP)
            reach = (t + 1) * STRIP
            seen = pl.ds(b * BLOCK, reach)
            k, v = rbuf[hl, 0, seen, :], rbuf[hl, 1, seen, :]
            q, g = rbuf[hl, 2, rows, :], rbuf[hl, 3, rows, :]
            mask = t * STRIP + lax.broadcasted_iota(
                jnp.int32, (STRIP, reach), 0
            ) >= lax.broadcasted_iota(jnp.int32, (STRIP, reach), 1)
            score = jnp.where(mask, dot(q, k, NT), 0.0).astype(BF16)
            grad_score = jnp.where(mask, dot(g, v, NT), 0.0).astype(BF16)
            part[0, rows, :] = dot(score, v, NN)
            part[1, rows, :] = dot(grad_score, k, NN)
            grad_key = dot(grad_score, q, TN)
            grad_value = dot(score, g, TN)
            if t:
                first = pl.ds(b * BLOCK, STRIP)
                part[2, first, :] += grad_key[:STRIP]
                part[3, first, :] += grad_value[:STRIP]
            part[2, rows, :] = grad_key[t * STRIP :]
            part[3, rows, :] = grad_value[t * STRIP :]

    def head(hl, carry):
        for a in (0, 1):
            for d in FAR_FIRST:
                z_copy(hl, a, d).wait_recv()
        local_copy(hl).wait()
        for b in range(2):
            rows = pl.ds(b * BLOCK, BLOCK)
            own[b] = dot(rbuf[hl, 0, rows, :], rbuf[hl, 1, rows, :], TN)
        for a in (2, 3):
            for d in FAR_FIRST:
                z_copy(hl, a, d).wait_recv()
        for b in range(2):
            rows = pl.ds(b * BLOCK, BLOCK)
            own[2 + b] = dot(rbuf[hl, 2, rows, :], rbuf[hl, 3, rows, :], TN)
        csend[hl, 0] = (own[0, other, :] + own[1, other, :]).astype(BF16)
        csend[hl, 1] = (own[2, other, :] + own[3, other, :]).astype(BF16)
        c_copy(hl).start()
        own_kv = own[0, mine, :] + own[1, mine, :]
        own_qg = own[2, mine, :] + own[3, mine, :]
        c_copy(hl).wait_recv()
        chip_kv = own_kv + cbuf[hl, 0].astype(F32)
        chip_qg = own_qg + cbuf[hl, 1].astype(F32)
        ysend[hl, 0] = chip_kv.astype(BF16)
        ysend[hl, 1] = chip_qg.astype(BF16)
        for d in (2, 1, 3):
            y_copy(hl, d).start()
        within_block(hl, 0)
        for d in (1, 3, 2):
            y_copy(hl, d).wait_recv()
        row_kv = own[0, mine, :] + own[1, mine, :] + cbuf[hl, 0].astype(F32)
        row_qg = own[2, mine, :] + own[3, mine, :] + cbuf[hl, 1].astype(F32)
        for d in (1, 2, 3):
            source = lax.rem(y + d, NY)
            row_kv = row_kv + ybuf[hl, source, 0].astype(F32)
            row_qg = row_qg + ybuf[hl, source, 1].astype(F32)
        xsend[hl, 0] = row_kv.astype(BF16)
        xsend[hl, 1] = row_qg.astype(BF16)
        for d in (2, 1, 3):
            x_copy(hl, d).start()
        within_block(hl, 1)
        before = jnp.zeros((HALF, 128), F32)
        after = jnp.zeros((HALF, 128), F32)
        for d in (1, 2, 3):
            source = lax.rem(y + d, NY)
            before = before + jnp.where(source < y, ybuf[hl, source, 0].astype(F32), 0.0)
            after = after + jnp.where(source > y, ybuf[hl, source, 1].astype(F32), 0.0)
        for d in (1, 3, 2):
            x_copy(hl, d).wait_recv()
        for d in (1, 2, 3):
            source = lax.rem(x + d, NX)
            got = xbuf[hl, source].astype(F32)
            before = before + jnp.where(source < x, got, 0.0)
            after = after + jnp.where(source > x, got, 0.0)
        own_kv = own[0, mine, :] + own[1, mine, :]
        own_qg = own[2, mine, :] + own[3, mine, :]
        fsend[hl, 0] = (before + jnp.where(core == 0, own_kv, 0.0)).astype(BF16)
        fsend[hl, 1] = (after + jnp.where(core == 1, own_qg, 0.0)).astype(BF16)
        f_copy(hl).start()
        before = before + jnp.where(core == 1, cbuf[hl, 0].astype(F32), 0.0)
        after = after + jnp.where(core == 0, cbuf[hl, 1].astype(F32), 0.0)
        before_used[0, mine, :] = before.astype(BF16)
        before_used[1, mine, :] = (before + own[0, mine, :]).astype(BF16)
        after_used[0, mine, :] = (after + own[3, mine, :]).astype(BF16)
        after_used[1, mine, :] = after.astype(BF16)
        f_copy(hl).wait_recv()
        before = fbuf[hl, 0].astype(F32)
        after = fbuf[hl, 1].astype(F32)
        before_used[0, other, :] = fbuf[hl, 0]
        before_used[1, other, :] = (before + own[0, other, :]).astype(BF16)
        after_used[0, other, :] = (after + own[3, other, :]).astype(BF16)
        after_used[1, other, :] = fbuf[hl, 1]
        for b in range(2):
            rows = pl.ds(b * BLOCK, BLOCK)
            to = pl.ds(b * BLOCK * 4 + hl, BLOCK, stride=4)
            k, v, q, g = (rbuf[hl, a, rows, :] for a in range(4))
            out_ref[0, to, :] = (dot(q, before_used[b], NN) + part[0, rows, :]) * recip_out[rows, :]
            out_ref[1, to, :] = dot(g, before_used[b], NT) + part[1, rows, :]
            out_ref[2, to, :] = dot(v, after_used[b], NT) + part[2, rows, :]
            out_ref[3, to, :] = dot(k, after_used[b], NN) + part[3, rows, :]
        return carry

    lax.fori_loop(0, 4, head, 0)

    def settle(hl, carry):
        for a in range(4):
            for d in FAR_FIRST:
                z_copy(hl, a, d).wait_send()
        c_copy(hl).wait_send()
        f_copy(hl).wait_send()
        for d in (1, 2, 3):
            y_copy(hl, d).wait_send()
            x_copy(hl, d).wait_send()
        return carry

    lax.fori_loop(0, 4, settle, 0)


def exchange(queries, keys_in, values, cotangent):
    flat = [
        pltpu.with_memory_space_constraint(a.reshape(ROWS * 32, 128), pltpu.HBM)
        for a in (queries, keys_in, values, cotangent)
    ]
    dma = pltpu.SemaphoreType.DMA
    return pl.pallas_call(
        exchange_kernel,
        out_shape=jax.ShapeDtypeStruct((4, 4096, 128), F32),
        in_specs=[pl.BlockSpec(memory_space=pl.ANY)] * 4,
        out_specs=pl.BlockSpec(memory_space=pltpu.VMEM),
        scratch_shapes=[
            pltpu.VMEM((4, ROWS * 32, 128), BF16),
            pltpu.VMEM((4, ROWS * 32, 128), F32),
            pltpu.VMEM((4, NZ, 4, ROWS, 128), BF16),
            pltpu.VMEM((4, 4, 1024, 128), BF16),
            pltpu.VMEM((ROWS, 128), F32),
            pltpu.VMEM((1024, 128), F32),
            pltpu.VMEM((4, 128, 128), F32),
            pltpu.VMEM((4, 1024, 128), F32),
            pltpu.VMEM((2, 128, 128), BF16),
            pltpu.VMEM((2, 128, 128), BF16),
            pltpu.VMEM((4, 2, HALF, 128), BF16),
            pltpu.VMEM((4, 2, HALF, 128), BF16),
            pltpu.VMEM((4, 2, HALF, 128), BF16),
            pltpu.VMEM((4, NY, 2, HALF, 128), BF16),
            pltpu.VMEM((4, 2, HALF, 128), BF16),
            pltpu.VMEM((4, NX, HALF, 128), BF16),
            pltpu.VMEM((4, 2, HALF, 128), BF16),
            pltpu.VMEM((4, 2, HALF, 128), BF16),
            dma((4,)), dma((4, 4, NZ)), dma((4, 4, NZ)), dma((4,)),
            dma((4,)), dma((4,)), dma((4, 4)), dma((4, 4)), dma((4, 4)), dma((4, 4)),
            dma((4,)), dma((4,)),
        ],
        compiler_params=pltpu.CompilerParams(
            collective_id=0, has_side_effects=True, vmem_limit_bytes=36 << 20
        ),
        name="exchange",
    )(*flat)


def pack_kernel(wide_ref, *refs):
    outs, narrow, sem = refs[:4], refs[4], refs[5]
    copies = []
    for c in range(4):
        for a in range(4):
            rows = pl.ds(c * 1024, 1024)
            narrow[a, rows, :] = wide_ref[a, rows, :].astype(BF16)
            copy = pltpu.make_async_copy(narrow.at[a, rows, :], outs[a].at[rows, :], sem.at[a, c])
            copy.start()
            copies.append(copy)
    for copy in copies:
        copy.wait()


def pack(wide):
    out = jax.ShapeDtypeStruct((4096, 128), BF16)
    results = pl.pallas_call(
        pack_kernel,
        out_shape=(out,) * 4,
        in_specs=[pl.BlockSpec(memory_space=pltpu.VMEM)],
        out_specs=(pl.BlockSpec(memory_space=pl.ANY),) * 4,
        scratch_shapes=[pltpu.VMEM((4, 4096, 128), BF16), pltpu.SemaphoreType.DMA((4, 4))],
        compiler_params=pltpu.CompilerParams(vmem_limit_bytes=16 << 20),
        name="pack",
    )(wide)
    return tuple(r.reshape(1024, 4, 128) for r in results)


def shards(queries, keys_in, values, cotangent):
    return pack(exchange(queries, keys_in, values, cotangent))


def solution(mesh):
    in_specs = (P(("seq", "head"), None, None),) * 4
    out_specs = (P("seq", "head", None),) * 4
    return jax.shard_map(shards, mesh=mesh, in_specs=in_specs, out_specs=out_specs, check_vma=False)
```

time: 130 us -> 118 us (0.908)
  the two profiles are of different devices: /device:TPU:7 before, /device:TPU:1 now
where the time goes in v2:
time: 118 us
  Pallas kernels  117 us (99%)
    pallas_call x1, Pallas kernels, exchange(): pl.pallas_call(exchange_kernel, out_shape=jax.ShapeDtypeStruct((4, 4096,...  115 us

profile of v2, /device:TPU:1, one launch (start us, length us, event | category | flops | bytes accessed | tf_op | source)
XLA Modules:
  0.0 118.2 jit_solution(4309813516189243692)
XLA Ops:
  0.6 115.3 %exchange.1.wide_ref = f32[4,4096,128]{2,1,0:T(8,128)S(1)} custom-call(bf16[4096,128]{1,0:T(8,128)(2,1)} %bitcast.8, bf16[4096,128]{1,0:T(8,128)(2,1)} %bitcast.9, bf16[4096,128]{1,0:T(8,128)(2,1)} %bitcast.10, bf16[4096,128]{1,0:T(8,128)(2,1)} %bitcast.11), custom_call_target="tpu_custom_call" | custom-call | tf_op jit(solution)/shard_map/exchange/pallas_call | solution.py:274
  115.9 2.2 %pack.1 = (bf16[4096,128]{1,0:T(8,128)(2,1)}, bf16[4096,128]{1,0:T(8,128)(2,1)}, bf16[4096,128]{1,0:T(8,128)(2,1)}, bf16[4096,128]{1,0:T(8,128)(2,1)}) custom-call(f32[4,4096,128]{2,1,0:T(8,128)S(1)} %exchange.1.wide_ref), custom_call_target="tpu_custom_call" | custom-call | tf_op jit(solution)/shard_map/pack/pallas_call | solution.py:325

commit v3 on v2

v3 whole, which is shorter than its diff:
```python
import functools

import jax
import jax.numpy as jnp
from jax import lax
from jax.experimental import pallas as pl
from jax.experimental.pallas import tpu as pltpu
from jax.sharding import PartitionSpec as P

BLOCK = 512
OFFSET = 1048576
MESH = pl.DeviceIdType.MESH
NZ = 8
NX = 4
ROWS = 128
HALF = 64
STRIP = 256
FAR_FIRST = (4, 3, 5, 2, 6, 1, 7)
ROW_ORDER = ((2, 0), (2, 1), (1, 0), (1, 1), (3, 0), (3, 1), (0, 1))
F32 = jnp.float32
BF16 = jnp.bfloat16


def dot(a, b, dims):
    return lax.dot_general(a, b, (dims, ((), ())), preferred_element_type=F32)


NN = ((1,), (0,))
NT = ((1,), (1,))
TN = ((0,), (0,))


def exchange_kernel(
    q_ref, k_ref, v_ref, g_ref, out_ref,
    inb, stg, sbuf, rbuf, recip, recip_out, own, part, state_used,
    half_send, row_buf, total_send, total_buf, pair_send, pair_buf,
    in_sem, s_sem, r_sem, l_sem, hs_sem, hr_sem, ts_sem, tr_sem, ps_sem, pr_sem,
):
    z = lax.axis_index("head")
    seq = lax.axis_index("seq")
    core = lax.rem(seq, 2)
    x = seq // 8
    place = lax.rem(seq, 8)
    row_start = x * 8
    partner = seq + 1 - 2 * core

    def row_peer(d, flip):
        return lax.rem(place - core + 2 * d, 8) + (1 - core if flip else core)

    inputs = (q_ref, g_ref, k_ref, v_ref)

    def load(a):
        return pltpu.make_async_copy(inputs[a], inb.at[a], in_sem.at[a])

    load(0).start()

    barrier = pltpu.get_barrier_semaphore()
    for d in range(1, NZ):
        pl.semaphore_signal(
            barrier, inc=1, device_id={"head": lax.rem(z + d, NZ)}, device_id_type=MESH
        )
    row_peers = [row_start + row_peer(d, flip) for d, flip in ROW_ORDER]
    x_peers = [
        lax.rem(x + d, NX) * 8 + place - core + c
        for d in (2, 1, 3) for c in range(2)
    ]
    for peer in row_peers + x_peers:
        pl.semaphore_signal(barrier, inc=1, device_id={"seq": peer}, device_id_type=MESH)

    first_row = (seq * NZ + z) * ROWS + OFFSET + 1
    position = (first_row + lax.broadcasted_iota(jnp.int32, (ROWS, 128), 0)).astype(F32)
    recip[...] = 1.0 / position

    def head_major(hl, a):
        for dest in range(NZ):
            piece = stg[a, pl.ds(dest * 4 + hl, ROWS, stride=32), :]
            if a == 1:
                piece = piece * recip[...]
            sbuf[hl, dest, a] = piece.astype(BF16)

    here = pl.ds(pl.multiple_of(z * ROWS, ROWS), ROWS)

    def z_copy(hl, st, d):
        dest = lax.rem(z + d, NZ)
        return pltpu.make_async_remote_copy(
            src_ref=sbuf.at[hl, dest, pl.ds(2 * st, 2)],
            dst_ref=rbuf.at[hl, pl.ds(2 * st, 2), here, :],
            send_sem=s_sem,
            recv_sem=r_sem.at[hl, st],
            device_id={"head": dest},
            device_id_type=MESH,
        )

    def local_copy(hl):
        return pltpu.make_async_copy(sbuf.at[hl, z], rbuf.at[hl, :, here, :], l_sem.at[hl])

    load(0).wait()
    for a in range(1, 4):
        load(a).start()
    for hl in range(4):
        for a in range(4):
            if hl == 0:
                if a:
                    load(a).wait()
                stg[a] = inb[a].astype(F32)
            head_major(hl, a)
            if hl == 0 and a == 1:
                pl.semaphore_wait(barrier, 20)
            if a % 2:
                for d in FAR_FIRST:
                    z_copy(hl, a // 2, d).start()
        local_copy(hl).start()

    position = (
        seq * 1024 + OFFSET + 1 + lax.broadcasted_iota(jnp.int32, (1024, 128), 0)
    ).astype(F32)
    recip_out[...] = 1.0 / position

    def half_copy(hl, st, d, flip):
        to = row_peer(d, flip)
        return pltpu.make_async_remote_copy(
            src_ref=half_send.at[hl, st, lax.rem(to, 2)],
            dst_ref=row_buf.at[hl, st, place],
            send_sem=hs_sem,
            recv_sem=hr_sem.at[hl, st],
            device_id={"seq": row_start + to},
            device_id_type=MESH,
        )

    def total_copy(hl, st, d, c):
        return pltpu.make_async_remote_copy(
            src_ref=total_send.at[hl, st],
            dst_ref=total_buf.at[hl, st, x, core],
            send_sem=ts_sem,
            recv_sem=tr_sem.at[hl, st, d - 1],
            device_id={"seq": lax.rem(x + d, NX) * 8 + place - core + c},
            device_id_type=MESH,
        )

    def pair_copy(hl, st):
        return pltpu.make_async_remote_copy(
            src_ref=pair_send.at[hl, st],
            dst_ref=pair_buf.at[hl, st],
            send_sem=ps_sem,
            recv_sem=pr_sem.at[hl, st],
            device_id={"seq": partner},
            device_id_type=MESH,
        )

    def wait_bytes(ref, sem):
        pltpu.make_async_copy(ref, ref, sem).wait()

    def goes(st, d):
        to = lax.rem(x + d, NX)
        return to < x if st == 0 else to > x

    def comes(st, d):
        source = lax.rem(x + NX - d, NX)
        return source > x if st == 0 else source < x

    mine = pl.ds(pl.multiple_of(core * HALF, HALF), HALF)
    other = pl.ds(pl.multiple_of((1 - core) * HALF, HALF), HALF)

    def within_block(hl, b):
        for t in range(2):
            rows = pl.ds(b * BLOCK + t * STRIP, STRIP)
            reach = (t + 1) * STRIP
            seen = pl.ds(b * BLOCK, reach)
            q, g = rbuf[hl, 0, rows, :], rbuf[hl, 1, rows, :]
            k, v = rbuf[hl, 2, seen, :], rbuf[hl, 3, seen, :]
            mask = t * STRIP + lax.broadcasted_iota(
                jnp.int32, (STRIP, reach), 0
            ) >= lax.broadcasted_iota(jnp.int32, (STRIP, reach), 1)
            score = jnp.where(mask, dot(q, k, NT), 0.0).astype(BF16)
            grad_score = jnp.where(mask, dot(g, v, NT), 0.0).astype(BF16)
            part[0, rows, :] = dot(score, v, NN)
            part[1, rows, :] = dot(grad_score, k, NN)
            grad_key = dot(grad_score, q, TN)
            grad_value = dot(score, g, TN)
            if t:
                first = pl.ds(b * BLOCK, STRIP)
                part[2, first, :] += grad_key[:STRIP]
                part[3, first, :] += grad_value[:STRIP]
            part[2, rows, :] = grad_key[t * STRIP :]
            part[3, rows, :] = grad_value[t * STRIP :]

    def own_states(hl, st):
        for b in range(2):
            rows = pl.ds(b * BLOCK, BLOCK)
            own[2 * st + b] = dot(rbuf[hl, 2 * st, rows, :], rbuf[hl, 2 * st + 1, rows, :], TN)
        for c in range(2):
            half = pl.ds(c * HALF, HALF)
            half_send[hl, st, c] = (own[2 * st, half, :] + own[2 * st + 1, half, :]).astype(BF16)
        for d, flip in ROW_ORDER:
            half_copy(hl, st, d, flip).start()

    def row_sums(hl, st):
        wait_bytes(row_buf.at[hl, st, pl.ds(0, 7)], hr_sem.at[hl, st])
        total = own[2 * st, mine, :] + own[2 * st + 1, mine, :]
        first = place - core
        here_sum = jnp.zeros((HALF, 128), F32)
        for d, flip in ROW_ORDER:
            source = row_peer(d, flip)
            got = row_buf[hl, st, source].astype(F32)
            if d:
                outside = source > first + 1 if st == 0 else source < first
                here_sum = here_sum + jnp.where(outside, got, 0.0)
            total = total + got
        total_send[hl, st] = total.astype(BF16)
        for d in (2, 1, 3):
            @pl.when(goes(st, d))
            def _():
                for c in range(2):
                    total_copy(hl, st, d, c).start()
        lone = own[2 * st, mine, :] + own[2 * st + 1, mine, :]
        pair = row_buf[hl, st, row_peer(0, 1)].astype(F32)
        takes = core == st
        pair_send[hl, st] = (here_sum + jnp.where(takes, 0.0, lone)).astype(BF16)
        pair_copy(hl, st).start()
        own[4 + st, mine, :] = here_sum + jnp.where(takes, pair, 0.0)

    def finish_state(hl, st):
        wait_bytes(pair_buf.at[hl, st], pr_sem.at[hl, st])
        own[4 + st, other, :] = pair_buf[hl, st].astype(F32)
        for d in (1, 3, 2):
            @pl.when(comes(st, d))
            def _():
                source = lax.rem(x + NX - d, NX)
                wait_bytes(total_buf.at[hl, st, source], tr_sem.at[hl, st, d - 1])
                for c in range(2):
                    half = pl.ds(c * HALF, HALF)
                    own[4 + st, half, :] += total_buf[hl, st, source, c].astype(F32)
        outer = own[4 + st]
        state_used[st, 1 - st] = outer.astype(BF16)
        state_used[st, st] = (outer + own[1 + st]).astype(BF16)

    def wait_rows(hl, st):
        wait_bytes(rbuf.at[hl, pl.ds(0, 2), pl.ds(0, 7 * ROWS)], r_sem.at[hl, st])

    def head(hl, carry):
        wait_rows(hl, 0)
        local_copy(hl).wait()
        own_states(hl, 0)
        row_sums(hl, 0)
        finish_state(hl, 0)
        wait_rows(hl, 1)
        own_states(hl, 1)
        within_block(hl, 0)
        within_block(hl, 1)
        row_sums(hl, 1)
        for b in range(2):
            rows = pl.ds(b * BLOCK, BLOCK)
            to = pl.ds(b * BLOCK * 4 + hl, BLOCK, stride=4)
            k, v = rbuf[hl, 2, rows, :], rbuf[hl, 3, rows, :]
            state = state_used[0, b]
            out_ref[2, to, :] = dot(v, state, NT) + part[2, rows, :]
            out_ref[3, to, :] = dot(k, state, NN) + part[3, rows, :]
        finish_state(hl, 1)
        for b in range(2):
            rows = pl.ds(b * BLOCK, BLOCK)
            to = pl.ds(b * BLOCK * 4 + hl, BLOCK, stride=4)
            q, g = rbuf[hl, 0, rows, :], rbuf[hl, 1, rows, :]
            state = state_used[1, b]
            out_ref[0, to, :] = (dot(q, state, NN) + part[0, rows, :]) * recip_out[rows, :]
            out_ref[1, to, :] = dot(g, state, NT) + part[1, rows, :]
        return carry

    lax.fori_loop(0, 4, head, 0)

    wait_bytes(sbuf.at[:, pl.ds(0, 7)], s_sem)
    wait_bytes(row_buf.at[:, :, pl.ds(0, 7)], hs_sem)
    wait_bytes(total_buf.at[:, 0, pl.ds(0, 3)], ts_sem)
    wait_bytes(pair_buf, ps_sem)


def exchange(queries, keys_in, values, cotangent):
    flat = [
        pltpu.with_memory_space_constraint(a.reshape(ROWS * 32, 128), pltpu.HBM)
        for a in (queries, keys_in, values, cotangent)
    ]
    dma = pltpu.SemaphoreType.DMA
    return pl.pallas_call(
        exchange_kernel,
        out_shape=jax.ShapeDtypeStruct((4, 4096, 128), F32),
        in_specs=[pl.BlockSpec(memory_space=pl.ANY)] * 4,
        out_specs=pl.BlockSpec(memory_space=pltpu.VMEM),
        scratch_shapes=[
            pltpu.VMEM((4, ROWS * 32, 128), BF16),
            pltpu.VMEM((4, ROWS * 32, 128), F32),
            pltpu.VMEM((4, NZ, 4, ROWS, 128), BF16),
            pltpu.VMEM((4, 4, 1024, 128), BF16),
            pltpu.VMEM((ROWS, 128), F32),
            pltpu.VMEM((1024, 128), F32),
            pltpu.VMEM((6, 128, 128), F32),
            pltpu.VMEM((4, 1024, 128), F32),
            pltpu.VMEM((2, 2, 128, 128), BF16),
            pltpu.VMEM((4, 2, 2, HALF, 128), BF16),
            pltpu.VMEM((4, 2, 8, HALF, 128), BF16),
            pltpu.VMEM((4, 2, HALF, 128), BF16),
            pltpu.VMEM((4, 2, NX, 2, HALF, 128), BF16),
            pltpu.VMEM((4, 2, HALF, 128), BF16),
            pltpu.VMEM((4, 2, HALF, 128), BF16),
            dma((4,)), dma, dma((4, 2)), dma((4,)),
            dma, dma((4, 2)), dma, dma((4, 2, 3)), dma, dma((4, 2)),
        ],
        compiler_params=pltpu.CompilerParams(
            collective_id=0, has_side_effects=True, vmem_limit_bytes=36 << 20
        ),
        name="exchange",
    )(*flat)


def pack_kernel(wide_ref, *refs):
    outs, narrow, sem = refs[:4], refs[4], refs[5]
    copies = []
    for c in range(4):
        for a in range(4):
            rows = pl.ds(c * 1024, 1024)
            narrow[a, rows, :] = wide_ref[a, rows, :].astype(BF16)
            copy = pltpu.make_async_copy(narrow.at[a, rows, :], outs[a].at[rows, :], sem.at[a, c])
            copy.start()
            copies.append(copy)
    for copy in copies:
        copy.wait()


def pack(wide):
    out = jax.ShapeDtypeStruct((4096, 128), BF16)
    results = pl.pallas_call(
        pack_kernel,
        out_shape=(out,) * 4,
        in_specs=[pl.BlockSpec(memory_space=pltpu.VMEM)],
        out_specs=(pl.BlockSpec(memory_space=pl.ANY),) * 4,
        scratch_shapes=[pltpu.VMEM((4, 4096, 128), BF16), pltpu.SemaphoreType.DMA((4, 4))],
        compiler_params=pltpu.CompilerParams(vmem_limit_bytes=16 << 20),
        name="pack",
    )(wide)
    return tuple(r.reshape(1024, 4, 128) for r in results)


def shards(queries, keys_in, values, cotangent):
    return pack(exchange(queries, keys_in, values, cotangent))


def solution(mesh):
    in_specs = (P(("seq", "head"), None, None),) * 4
    out_specs = (P("seq", "head", None),) * 4
    return jax.shard_map(shards, mesh=mesh, in_specs=in_specs, out_specs=out_specs, check_vma=False)
```

time: 118 us -> 112 us (0.949)
  the two profiles are of different devices: /device:TPU:1 before, /device:TPU:7 now
where the time goes in v3:
time: 112 us
  Pallas kernels  111 us (99%)
    pallas_call x1, Pallas kernels, exchange(): pl.pallas_call(exchange_kernel, out_shape=jax.ShapeDtypeStruct((4, 4096,...  109 us

profile of v3, /device:TPU:7, one launch (start us, length us, event | category | flops | bytes accessed | tf_op | source)
XLA Modules:
  0.0 112.1 jit_solution(2357829422683346915)
XLA Ops:
  0.6 109.3 %exchange.1.wide_ref = f32[4,4096,128]{2,1,0:T(8,128)S(1)} custom-call(bf16[4096,128]{1,0:T(8,128)(2,1)} %bitcast.8, bf16[4096,128]{1,0:T(8,128)(2,1)} %bitcast.9, bf16[4096,128]{1,0:T(8,128)(2,1)} %bitcast.10, bf16[4096,128]{1,0:T(8,128)(2,1)} %bitcast.11), custom_call_target="tpu_custom_call" | custom-call | tf_op jit(solution)/shard_map/exchange/pallas_call | solution.py:282
  110.0 2.2 %pack.1 = (bf16[4096,128]{1,0:T(8,128)(2,1)}, bf16[4096,128]{1,0:T(8,128)(2,1)}, bf16[4096,128]{1,0:T(8,128)(2,1)}, bf16[4096,128]{1,0:T(8,128)(2,1)}) custom-call(f32[4,4096,128]{2,1,0:T(8,128)S(1)} %exchange.1.wide_ref), custom_call_target="tpu_custom_call" | custom-call | tf_op jit(solution)/shard_map/pack/pallas_call | solution.py:329

commit v4 on v3

--- a/solution.py
+++ b/solution.py
@@ -16,6 +16,7 @@
 HALF = 64
 STRIP = 256
 FAR_FIRST = (4, 3, 5, 2, 6, 1, 7)
+PLANES = (0, 1, 2, 3, 7, 4, 6, 5)
 ROW_ORDER = ((2, 0), (2, 1), (1, 0), (1, 1), (3, 0), (3, 1), (0, 1))
 F32 = jnp.float32
 BF16 = jnp.bfloat16
@@ -107,8 +108,14 @@
             if hl == 0 and a == 1:
                 pl.semaphore_wait(barrier, 20)
             if a % 2:
-                for d in FAR_FIRST:
-                    z_copy(hl, a // 2, d).start()
+                if hl < 3 or a < 1:
+                    for d in FAR_FIRST:
+                        z_copy(hl, a // 2, d).start()
+                else:
+                    for dest in PLANES:
+                        @pl.when(dest != z)
+                        def _():
+                            z_copy(hl, a // 2, lax.rem(dest + NZ - z, NZ)).start()
         local_copy(hl).start()
 
     position = (

time: 112 us -> 111 us (level); the launches traced: 112 us -> 110 us
  Pallas kernels: 111 us -> 109 us
    pallas_call x1, Pallas kernels: 109 us -> 107 us  [exchange(): pl.pallas_call(exchange_kernel, out_shape=jax.ShapeDtypeStruct((4, 4096,...]
where the time goes in v4:
time: 111 us; the launch traced here: 110 us
  Pallas kernels  109 us (98%)
    pallas_call x1, Pallas kernels, exchange(): pl.pallas_call(exchange_kernel, out_shape=jax.ShapeDtypeStruct((4, 4096,...  107 us

profile of v4, /device:TPU:7, one launch (start us, length us, event | category | flops | bytes accessed | tf_op | source)
XLA Modules:
  0.0 109.6 jit_solution(9987462706167625205)
XLA Ops:
  0.6 106.8 %exchange.1.wide_ref = f32[4,4096,128]{2,1,0:T(8,128)S(1)} custom-call(bf16[4096,128]{1,0:T(8,128)(2,1)} %bitcast.8, bf16[4096,128]{1,0:T(8,128)(2,1)} %bitcast.9, bf16[4096,128]{1,0:T(8,128)(2,1)} %bitcast.10, bf16[4096,128]{1,0:T(8,128)(2,1)} %bitcast.11), custom_call_target="tpu_custom_call" | custom-call | tf_op jit(solution)/shard_map/exchange/pallas_call | solution.py:289
  107.4 2.2 %pack.1 = (bf16[4096,128]{1,0:T(8,128)(2,1)}, bf16[4096,128]{1,0:T(8,128)(2,1)}, bf16[4096,128]{1,0:T(8,128)(2,1)}, bf16[4096,128]{1,0:T(8,128)(2,1)}) custom-call(f32[4,4096,128]{2,1,0:T(8,128)S(1)} %exchange.1.wide_ref), custom_call_target="tpu_custom_call" | custom-call | tf_op jit(solution)/shard_map/pack/pallas_call | solution.py:336

commit v5 on v4

--- a/solution.py
+++ b/solution.py
@@ -253,8 +253,8 @@
         wait_rows(hl, 1)
         own_states(hl, 1)
         within_block(hl, 0)
+        row_sums(hl, 1)
         within_block(hl, 1)
-        row_sums(hl, 1)
         for b in range(2):
             rows = pl.ds(b * BLOCK, BLOCK)
             to = pl.ds(b * BLOCK * 4 + hl, BLOCK, stride=4)

time: 111 us -> 111 us (level)
  no operation moved by 1% of the time
where the time goes in v5:
time: 111 us; the launch traced here: 110 us
  Pallas kernels  109 us (98%)
    pallas_call x1, Pallas kernels, exchange(): pl.pallas_call(exchange_kernel, out_shape=jax.ShapeDtypeStruct((4, 4096,...  107 us

profile of v5, /device:TPU:7, one launch (start us, length us, event | category | flops | bytes accessed | tf_op | source)
XLA Modules:
  0.0 109.6 jit_solution(9745004546017631607)
XLA Ops:
  0.6 106.8 %exchange.1.wide_ref = f32[4,4096,128]{2,1,0:T(8,128)S(1)} custom-call(bf16[4096,128]{1,0:T(8,128)(2,1)} %bitcast.8, bf16[4096,128]{1,0:T(8,128)(2,1)} %bitcast.9, bf16[4096,128]{1,0:T(8,128)(2,1)} %bitcast.10, bf16[4096,128]{1,0:T(8,128)(2,1)} %bitcast.11), custom_call_target="tpu_custom_call" | custom-call | tf_op jit(solution)/shard_map/exchange/pallas_call | solution.py:289
  107.4 2.2 %pack.1 = (bf16[4096,128]{1,0:T(8,128)(2,1)}, bf16[4096,128]{1,0:T(8,128)(2,1)}, bf16[4096,128]{1,0:T(8,128)(2,1)}, bf16[4096,128]{1,0:T(8,128)(2,1)}) custom-call(f32[4,4096,128]{2,1,0:T(8,128)S(1)} %exchange.1.wide_ref), custom_call_target="tpu_custom_call" | custom-call | tf_op jit(solution)/shard_map/pack/pallas_call | solution.py:336
